TPU v7x, 32 devices: a whole 2x2x4 slice. The times are simulated.
32 devices in a mesh: ctx: 4 (over y, x), exp: 8 (over z, core).
Axes of the slice: x: 2, y: 2, z: 4, core: 2. Of those that a mesh axis runs over, the one named last changes fastest.
Arguments:
- hidden_in: bfloat16 [1024, 2048], P(('ctx', 'exp')), may hold values from -6 to 6
- queries: bfloat16 [1024, 4096], P('ctx', 'exp'), may hold values from -200 to 200
- keyvals: bfloat16 [1024, 512], P('ctx'), may hold values from -6 to 6
- out_weight: bfloat16 [4096, 2048], P('exp'), may hold values from -0.09375 to 0.09375
- norm_gain: float32 [2048], replicated, may hold values from 0.5 to 1.5
- router_weight: bfloat16 [2048, 16], replicated, may hold values from -0.125 to 0.125
- expert_gate_up: bfloat16 [16, 2048, 1536], P('exp', 'ctx'), may hold values from -0.125 to 0.125
- expert_down: bfloat16 [16, 768, 2048], P('exp', 'ctx'), may hold values from -0.21875 to 0.21875
- route_ids: int32 [1024, 8], P(('ctx', 'exp')), may hold values from 0 to 15, all different within a row; in each aligned block of 32 rows (0 to 31, 32 to 63, ...) at most 18 rows name the same one
- upstream: bfloat16 [1024, 2048], P(('ctx', 'exp')), may hold values from -6 to 6
Outputs:
- layer_out: bfloat16 [1024, 2048], P(('ctx', 'exp'))
- input_grad: bfloat16 [1024, 2048], P(('ctx', 'exp'))
- query_grad: bfloat16 [1024, 4096], P('ctx', 'exp')
- out_weight_grad: float32 [4096, 2048], P('exp', 'ctx')
- gate_up_grad: float32 [16, 2048, 1536], P('exp', 'ctx')
- down_grad: float32 [16, 768, 2048], P('exp', 'ctx')
- router_grad: float32 [2048, 16], replicated
- gain_grad: float32 [2048], replicated
Inputs may be any that keep to these rules, and one draw needn't show every extreme that they name: `route_ids`: each row names 8 different experts. In each aligned block of 32 rows (the rows of one device) no expert is named by more than 18 rows, a bound that some block reaches.
All inputs are finite; a program needn't handle non-finite values.
Results may differ from a plain program's by a relative error of at most 0.02.
Values may be sent and summed in bfloat16 or wider, within the bound.
A program may use at most 128 MiB of HBM per device.

v0:
```python
import jax
import jax.numpy as jnp
from jax import lax
from jax.sharding import PartitionSpec as P

HEAD_WIDTH = 128
QUERY_HEADS = 32
KEY_VALUE_HEADS = 2
FFE = 768
EXPERTS = 16
norm_eps = 1e-06


def per_device(
    hidden_in,
    queries,
    keyvals,
    out_weight,
    norm_gain,
    router_weight,
    expert_gate_up,
    expert_down,
    route_ids,
    upstream,
):
    exp_count = lax.axis_size("exp")
    ctx_index = lax.axis_index("ctx")
    exp_index = lax.axis_index("exp")
    tok_ctx = queries.shape[0]
    tok_dev = hidden_in.shape[0]
    local_heads = queries.shape[1] // HEAD_WIDTH
    local_experts = EXPERTS // exp_count
    score_scale = HEAD_WIDTH ** (-0.5)
    keyvalue_head = exp_index * local_heads // (QUERY_HEADS // KEY_VALUE_HEADS)
    own_block = lax.dynamic_slice_in_dim(keyvals, keyvalue_head * 2 * HEAD_WIDTH, 2 * HEAD_WIDTH, 1)
    all_kv = lax.all_gather(own_block, "ctx", axis=0, tiled=True)
    ids_block = lax.all_gather(route_ids, "exp", axis=0, tiled=True)
    upstream_block = lax.all_gather(upstream, "exp", axis=0, tiled=True)
    gate_up_full = lax.all_gather(expert_gate_up, "ctx", axis=1, tiled=True)
    down_full = lax.all_gather(expert_down, "ctx", axis=1, tiled=True)
    upstream_all = lax.all_gather(upstream_block, "ctx", axis=0, tiled=True)
    keys, values = (all_kv[:, :HEAD_WIDTH], all_kv[:, HEAD_WIDTH:])
    query_pos = ctx_index * tok_ctx + jnp.arange(tok_ctx, dtype=jnp.int32)
    key_pos = jnp.arange(keys.shape[0], dtype=jnp.int32)
    allowed = key_pos[None, :] <= query_pos[:, None]

    def columns(array, head):
        return array[:, head * HEAD_WIDTH : (head + 1) * HEAD_WIDTH]

    def dot_t(a, b):
        return lax.dot_general(a, b, (((1,), (1,)), ((), ())), preferred_element_type=jnp.float32)

    def head_scores(head):
        return jnp.where(allowed, dot_t(columns(queries, head), keys) * score_scale, -jnp.inf)

    attention_heads, log_totals = ([], [])
    for head in range(local_heads):
        scores = head_scores(head)
        row_max = jnp.max(scores, axis=1, keepdims=True)
        weights = jnp.exp(scores - row_max)
        row_sum = jnp.sum(weights, axis=1, keepdims=True)
        mixed = jnp.dot(weights.astype(jnp.bfloat16), values, preferred_element_type=jnp.float32)
        attention_heads.append((mixed / row_sum).astype(jnp.bfloat16))
        log_totals.append(row_max + jnp.log(row_sum))
    attention_flat = jnp.concatenate(attention_heads, axis=1)
    attention_all = lax.all_gather(attention_flat, "ctx", axis=0, tiled=True)
    projected = lax.psum_scatter(
        jnp.dot(attention_flat, out_weight, preferred_element_type=jnp.float32).astype(
            jnp.bfloat16
        ),
        "exp",
        scatter_dimension=0,
        tiled=True,
    ).astype(jnp.float32)
    residual = hidden_in.astype(jnp.float32) + projected
    inv_rms = lax.rsqrt(jnp.mean(residual * residual, axis=1, keepdims=True) + norm_eps)
    normed = (residual * inv_rms * norm_gain).astype(jnp.bfloat16)
    normed_block = lax.all_gather(normed, "exp", axis=0, tiled=True)
    normed_cols = lax.all_to_all(normed_block, "ctx", split_axis=1, concat_axis=0, tiled=True)
    logits = jnp.dot(normed_block, router_weight, preferred_element_type=jnp.float32)
    expert_ids = jnp.arange(EXPERTS, dtype=jnp.int32)
    hit_block = jnp.any(ids_block[:, :, None] == expert_ids, axis=1)
    masked = jnp.where(hit_block, logits, -jnp.inf)
    shifted = jnp.exp(masked - jnp.max(masked, axis=1, keepdims=True))
    probs_block = shifted / jnp.sum(shifted, axis=1, keepdims=True)
    probs_here = lax.dynamic_slice_in_dim(probs_block, exp_index * local_experts, local_experts, 1)
    probs_cols = probs_here.T[:, :, None]
    out_grad_block = upstream_block.astype(jnp.float32)
    row_grads = (probs_cols * out_grad_block[None]).astype(jnp.bfloat16)
    gate_up = jnp.einsum(
        "td,edf->etf", normed_block, gate_up_full, preferred_element_type=jnp.float32
    )
    gate_part = gate_up[:, :, :FFE]
    up_part = gate_up[:, :, FFE:]
    sigmoid_gate = jax.nn.sigmoid(gate_part)
    activation = (gate_part * sigmoid_gate * up_part).astype(jnp.bfloat16)
    scaled_act = (probs_cols * activation.astype(jnp.float32)).astype(jnp.bfloat16)
    act_grad = jnp.einsum("etd,efd->etf", row_grads, down_full, preferred_element_type=jnp.float32)
    gate_grad = act_grad * up_part * sigmoid_gate * (1.0 + gate_part * (1.0 - sigmoid_gate))
    up_grad = act_grad * gate_part * sigmoid_gate
    pair_grad = jnp.concatenate([gate_grad, up_grad], axis=2).astype(jnp.bfloat16)
    pair_grad_all = lax.all_gather(pair_grad, "ctx", axis=1, tiled=True)
    rows_back = jnp.einsum(
        "etf,edf->td", pair_grad, gate_up_full, preferred_element_type=jnp.float32
    )
    expert_part = lax.psum_scatter(
        rows_back.astype(jnp.bfloat16), "exp", scatter_dimension=0, tiled=True
    ).astype(jnp.float32)
    expert_out = (
        jnp.einsum("etf,efd->etd", activation, down_full, preferred_element_type=jnp.float32)
        .astype(jnp.bfloat16)
        .astype(jnp.float32)
    )
    prob_grads_here = jnp.sum(expert_out * out_grad_block[None], axis=2)
    prob_grads = lax.all_to_all(prob_grads_here, "exp", split_axis=1, concat_axis=0, tiled=True).T
    mixture = lax.psum_scatter(
        jnp.sum(probs_cols * expert_out, axis=0).astype(jnp.bfloat16),
        "exp",
        scatter_dimension=0,
        tiled=True,
    ).astype(jnp.float32)
    layer_out = (residual + mixture).astype(jnp.bfloat16)
    act_rows = lax.all_to_all(
        jnp.swapaxes(scaled_act, 1, 2), "ctx", split_axis=1, concat_axis=2, tiled=True
    )
    down_grad = jnp.einsum(
        "eft,td->efd", act_rows, upstream_all, preferred_element_type=jnp.float32
    )
    gate_up_grad = jnp.einsum(
        "td,etf->edf", normed_cols, pair_grad_all, preferred_element_type=jnp.float32
    )
    out_grad = upstream.astype(jnp.float32)
    probs = lax.dynamic_slice_in_dim(probs_block, exp_index * tok_dev, tok_dev, 0)
    logit_grad = probs * (prob_grads - jnp.sum(probs * prob_grads, axis=1, keepdims=True))
    router_term = jnp.einsum(
        "te,td->ed", logit_grad, normed.astype(jnp.float32), precision=lax.Precision.HIGHEST
    )
    normed_grad = expert_part + jnp.einsum(
        "te,de->td", logit_grad, router_weight.astype(jnp.float32), precision=lax.Precision.HIGHEST
    )
    gain_term = jnp.sum(normed_grad * residual * inv_rms, axis=0, keepdims=True)
    summed = lax.psum(jnp.concatenate([router_term, gain_term], axis=0), ("ctx", "exp"))
    router_grad, gain_grad = (summed[:EXPERTS].T, summed[EXPERTS])
    inner_mean = jnp.mean(residual * norm_gain * normed_grad, axis=1, keepdims=True)
    input_grad = (
        out_grad + norm_gain * inv_rms * normed_grad - residual * inv_rms**3 * inner_mean
    ).astype(jnp.bfloat16)
    arriving = lax.all_gather(input_grad, "exp", axis=0, tiled=True)
    arriving_cols = lax.all_to_all(arriving, "ctx", split_axis=1, concat_axis=0, tiled=True)
    out_weight_grad = jnp.einsum(
        "tc,td->cd", attention_all, arriving_cols, preferred_element_type=jnp.float32
    )
    attention_grad = dot_t(arriving, out_weight).astype(jnp.bfloat16)
    query_grads = []
    for head in range(local_heads):
        grad_head = columns(attention_grad, head)
        delta = jnp.sum(
            grad_head.astype(jnp.float32) * attention_heads[head].astype(jnp.float32),
            axis=1,
            keepdims=True,
        )
        attn_probs = jnp.exp(head_scores(head) - log_totals[head])
        score_grad = (attn_probs * (dot_t(grad_head, values) - delta)).astype(jnp.bfloat16)
        query_acc = jnp.dot(score_grad, keys, preferred_element_type=jnp.float32)
        query_grads.append((score_scale * query_acc).astype(jnp.bfloat16))
    query_grad = jnp.concatenate(query_grads, axis=1)
    return (
        layer_out,
        input_grad,
        query_grad,
        out_weight_grad,
        gate_up_grad,
        down_grad,
        router_grad,
        gain_grad,
    )


def solution(mesh):
    return jax.shard_map(
        per_device,
        mesh=mesh,
        in_specs=(
            P(("ctx", "exp"), None),
            P("ctx", "exp"),
            P("ctx", None),
            P("exp", None),
            P(),
            P(),
            P("exp", "ctx", None),
            P("exp", "ctx", None),
            P(("ctx", "exp"), None),
            P(("ctx", "exp"), None),
        ),
        out_specs=(
            P(("ctx", "exp"), None),
            P(("ctx", "exp"), None),
            P("ctx", "exp"),
            P("exp", "ctx"),
            P("exp", "ctx", None),
            P("exp", "ctx", None),
            P(),
            P(),
        ),
        check_vma=False,
    )
```

profile of v0, /device:TPU:0, one launch (start us, length us, event | category | flops | bytes accessed | tf_op | source)
XLA Modules:
  0.0 746.0 jit_solution(9986827355923564355)
XLA Ops:
  8.3 11.5 %all_gather.30 = bf16[1024,256]{1,0:T(8,128)(2,1)S(1)} all-gather(bf16[256,256]{1,0:T(8,128)(2,1)S(1)} %constant_dynamic-slice_fusion), channel_id=1, replica_groups=mesh['ctx'=4,'exp'=8] {'ctx'}, dimensions={0}, use_global_device_ids=true | all-gather | bytes 655360 | tf_op jit(solution)/shard_map/all_gather | solution.py:36
  21.1 1.3 fusion.114
  25.8 1.7 convolution_convert_fusion.1
  28.3 32.2 %reduce-scatter.4.cloned.1.call-done = bf16[32,2048]{1,0:T(8,128)(2,1)} async-done(((bf16[256,2048]{1,0:T(8,128)(2,1)}), bf16[32,2048]{1,0:T(8,128)(2,1)}) %reduce-scatter.4.cloned.1.call-update) | async-done | bytes 131088 | tf_op jit(solution)/shard_map/reduce_scatter | solution.py:67
  62.2 1.6 multiply_convert_fusion.6
  65.1 14.4 %all-gather = s32[8,32,8]{1,2,0:T(8,128)S(1)} all-gather(s32[1,32,8]{1,2,0:T(8,128)S(1)} %bitcast.93), channel_id=1, replica_groups=mesh['ctx'=4,'exp'=8] {'exp'}, dimensions={0}, use_global_device_ids=true | all-gather | bytes 9216 | tf_op jit(solution)/shard_map/all_gather | solution.py:37
  79.6 2.9 all-gather.16.cloned.1.call-done
  82.5 2.8 convert_element_type.151
  85.3 21.3 %all-gather.10.cloned.1.call-done = bf16[256,2048]{1,0:T(8,128)(2,1)} async-done(((bf16[32,2048]{1,0:T(8,128)(2,1)}), bf16[256,2048]{1,0:T(8,128)(2,1)}) %all-gather.10.cloned.1.call-update) | async-done | bytes 1048592 | tf_op jit(solution)/shard_map/all_gather | solution.py:78
  106.6 1.6 fusion.116
  108.3 122.0 %all-gather.12.cloned.1.call-done = bf16[2,2048,1536]{2,1,0:T(8,128)(2,1)} async-done(((bf16[2,512,1536]{2,1,0:T(8,128)(2,1)}), bf16[2,2048,1536]{2,1,0:T(8,128)(2,1)}) %all-gather.12.cloned.1.call-update) | async-done | bytes 12582928 | tf_op jit(solution)/shard_map/all_gather | solution.py:39
  230.4 10.0 %convolution_bitcast_fusion.1 = f32[2,256,1536]{2,1,0:T(8,128)} fusion(bf16[2,2048,1536]{2,1,0:T(8,128)(2,1)} %all-gather.12.cloned.1.call-done, bf16[256,2048]{1,0:T(8,128)(2,1)} %all-gather.10.cloned.1.call-done), kind=kOutput, calls=%fused_computation.8 | convolution fusion | flops 3221225472 | bytes 16777216 | tf_op jit(solution)/shard_map/td,edf->etf/dot_general | solution.py:90
  240.3 61.8 %all-gather.14.cloned.1.call-done = bf16[2,768,2048]{2,1,0:T(8,128)(2,1)} async-done(((bf16[2,192,2048]{2,1,0:T(8,128)(2,1)}), bf16[2,768,2048]{2,1,0:T(8,128)(2,1)}) %all-gather.14.cloned.1.call-update) | async-done | bytes 6291472 | tf_op jit(solution)/shard_map/all_gather | solution.py:40
  302.1 9.5 %multiply_convert_fusion.4 = (bf16[2,256,768]{2,1,0:T(8,128)(2,1)S(1)}, bf16[2,256,768]{2,1,0:T(8,128)(2,1)S(1)}, bf16[2,768,256]{1,2,0:T(8,128)(2,1)}, bf16[2,256,768]{2,1,0:T(8,128)(2,1)}) fusion(f32[2,256,1536]{2,1,0:T(8,128)} %convolution_bitcast_fusion.1, f32[2,256]{1,0:T(2,128)S(1)} %dynamic-slice_bitcast_fusion, ...), kind=kOutput, calls=%fused_computation.20 | convolution fusion | flops 1620180992 | bytes 14684160 | tf_op jit(solution)/shard_map/etd,efd->etf/dot_general | solution.py:98
  312.4 9.0 %fusion.4 = bf16[256,2048]{1,0:T(8,128)(2,1)} fusion(bf16[2,2048,1536]{2,1,0:T(8,128)(2,1)} %all-gather.12.cloned.1.call-done, bf16[2,256,768]{2,1,0:T(8,128)(2,1)S(1)} %get-tuple-element.51, bf16[2,256,768]{2,1,0:T(8,128)(2,1)S(1)} %get-tuple-element.50), kind=kOutput, calls=%fused_computation.12 | convolution fusion | flops 3224895488 | bytes 15204352 | tf_op jit(solution)/shard_map/etf,edf->td/dot_general | solution.py:103
  321.5 7.0 fusion.1
  329.9 4.6 all-to-all-start
  334.6 5.6 all-to-all-done
  341.2 13.0 %reduce-scatter.8.cloned.1.call-done = bf16[32,2048]{1,0:T(8,128)(2,1)} async-done(((bf16[256,2048]{1,0:T(8,128)(2,1)}), bf16[32,2048]{1,0:T(8,128)(2,1)}) %reduce-scatter.8.cloned.1.call-update) | async-done | bytes 131088 | tf_op jit(solution)/shard_map/reduce_scatter | solution.py:106
  354.2 1.5 multiply_reduce_fusion
  356.2 1.6 pad_maximum_fusion.3
  357.9 30.1 %reduce-scatter.6.cloned.1.call-done = bf16[32,2048]{1,0:T(8,128)(2,1)} async-done(((bf16[256,2048]{1,0:T(8,128)(2,1)}), bf16[32,2048]{1,0:T(8,128)(2,1)}) %reduce-scatter.6.cloned.1.call-update) | async-done | bytes 131088 | tf_op jit(solution)/shard_map/reduce_scatter | solution.py:116
  388.0 1.8 subtract_convert_fusion
  389.9 1.6 pad_maximum_fusion.1
  391.6 2.4 pad_maximum_fusion
  394.6 3.1 copy.61
  397.7 4.4 all-to-all-start.3
  405.0 13.4 %all-to-all-done.3 = bf16[2,768,256]{2,0,1:T(2,128)(2,1)} async-done(((bf16[2,768,256]{2,0,1:T(2,128)(2,1)}), bf16[2,768,256]{2,0,1:T(2,128)(2,1)}, u32[]{:S(2)}, u32[]{:S(2)}) %all-to-all-start.3) | async-done | bytes 786464 | tf_op jit(solution)/shard_map/all_to_all | solution.py:123
  419.7 29.4 %all-gather.24.cloned.1.call-done = bf16[1024,2048]{1,0:T(8,128)(2,1)} async-done(((bf16[256,2048]{1,0:T(8,128)(2,1)}), bf16[1024,2048]{1,0:T(8,128)(2,1)}) %all-gather.24.cloned.1.call-update) | async-done | bytes 4194320 | tf_op jit(solution)/shard_map/all_gather | solution.py:41
  449.1 5.6 fusion.2
  454.8 125.2 %all-reduce.2.cloned.1.call-done = f32[17,2048]{1,0:T(8,128)} async-done(((f32[17,2048]{1,0:T(8,128)}), f32[17,2048]{1,0:T(8,128)}) %all-reduce.2.cloned.1.call-update) | async-done | bytes 139280 | tf_op jit(solution)/shard_map/psum | solution.py:142
  579.9 1.4 slice.69
  581.4 1.6 slice_bitcast_fusion
  583.0 22.2 %all-gather.18.cloned.1.call-done = bf16[256,2048]{1,0:T(8,128)(2,1)} async-done(((bf16[32,2048]{1,0:T(8,128)(2,1)}), bf16[256,2048]{1,0:T(8,128)(2,1)}) %all-gather.18.cloned.1.call-update) | async-done | bytes 1048592 | tf_op jit(solution)/shard_map/all_gather | solution.py:148
  605.2 2.3 copy.78
  607.5 4.4 all-to-all-start.1
  611.8 2.0 convolution_convert_fusion.2
  614.6 1.6 fusion.39
  616.2 2.0 fusion.38
  618.2 10.8 %all-to-all-done.1 = bf16[256,4,512]{2,0,1:T(8,128)(2,1)} async-done(((bf16[256,4,512]{2,0,1:T(8,128)(2,1)}), bf16[256,4,512]{2,0,1:T(8,128)(2,1)}, u32[]{:S(2)}, u32[]{:S(2)}) %all-to-all-start.1) | async-done | bytes 1048608 | tf_op jit(solution)/shard_map/all_to_all | solution.py:149
  629.0 4.2 all-to-all-start.2
  633.3 2.5 fusion.37
  635.8 2.2 fusion.36
  639.8 11.8 %all-gather.20.cloned.1.call-done = bf16[1024,512]{0,1:T(8,128)(2,1)} async-done(((bf16[256,512]{0,1:T(8,128)(2,1)}), bf16[1024,512]{0,1:T(8,128)(2,1)}) %all-gather.20.cloned.1.call-update) | async-done | bytes 1048592 | tf_op jit(solution)/shard_map/all_gather | solution.py:66
  651.6 3.2 fusion.117
  654.8 68.7 %all-gather.22.cloned.1.call-done = bf16[2,1024,1536]{2,1,0:T(8,128)(2,1)} async-done(((bf16[2,256,1536]{2,1,0:T(8,128)(2,1)}), bf16[2,1024,1536]{2,1,0:T(8,128)(2,1)}) %all-gather.22.cloned.1.call-update) | async-done | bytes 6291472 | tf_op jit(solution)/shard_map/all_gather | solution.py:102
  723.5 9.1 %convolution_bitcast_fusion = f32[2,512,1536]{1,2,0:T(8,128)} fusion(bf16[2,1024,1536]{2,1,0:T(8,128)(2,1)} %all-gather.22.cloned.1.call-done, bf16[1024,512,1]{1,0,2:T(8,128)(2,1)} %bitcast.18), kind=kOutput, calls=%fused_computation.2 | convolution fusion | flops 3221225472 | bytes 13631488 | tf_op jit(solution)/shard_map/td,etf->edf/dot_general | solution.py:129
  732.6 6.6 copy.65
  (147 shorter events, 20.7 us)
Async XLA Ops:
  7.2 18.6 %copy-start = (bf16[512,2048]{1,0:T(8,128)(2,1)S(1)}, bf16[512,2048]{1,0:T(8,128)(2,1)}, u32[]{:S(2)}) copy-start(bf16[512,2048]{1,0:T(8,128)(2,1)} %param.13) | copy-start | bytes 6291460
  7.2 15.2 %copy-start.42 = (bf16[256,512]{1,0:T(8,128)(2,1)S(1)}, bf16[256,512]{1,0:T(8,128)(2,1)}, u32[]{:S(2)}) copy-start(bf16[256,512]{1,0:T(8,128)(2,1)} %param.11) | copy-start | bytes 786436
  7.2 53.3 %reduce-scatter.4.cloned.1.call-start = ((), (), s32[]{:S(2)}) async-start(), calls=%async_computation.7 | async-start | bytes 1179648 | tf_op jit(solution)/shard_map/reduce_scatter | solution.py:67
  19.9 5.5 copy-start.16
  21.1 2.6 copy-start.9
  21.1 2.6 copy-start.31
  23.2 2.2 copy-start.5
  23.2 2.2 copy-start.29
  25.0 2.6 copy-start.12
  25.4 35.1 %copy-start.2 = (bf16[32,2048]{1,0:T(8,128)(2,1)S(1)}, bf16[32,2048]{1,0:T(8,128)(2,1)}, u32[]{:S(2)}) copy-start(bf16[32,2048]{1,0:T(8,128)(2,1)} %param.10) | copy-start | bytes 393220
  25.4 36.8 %copy-start.21 = (f32[2048]{0:T(1024)S(1)}, f32[2048]{0:T(1024)}, u32[]{:S(2)}) copy-start(f32[2048]{0:T(1024)} %param.14) | copy-start | bytes 24580
  25.8 38.7 %copy-start.14 = (bf16[256,128]{0,1:T(8,128)(2,1)}, bf16[256,128]{0,1:T(8,128)(2,1)S(1)}, u32[]{:S(2)}) copy-start(bf16[256,128]{0,1:T(8,128)(2,1)S(1)} %fusion.35) | copy-start | bytes 196612
  27.5 37.6 %copy-start.24 = (s32[32,8]{0,1:T(8,128)S(1)}, s32[32,8]{0,1:T(8,128)}, u32[]{:S(2)}) copy-start(s32[32,8]{0,1:T(8,128)} %param.18) | copy-start | bytes 3076
  27.5 55.0 %all-gather.16.cloned.1.call-start = ((), (), s32[]{:S(2)}) async-start(), calls=%async_computation.12 | async-start | bytes 1179648 | tf_op jit(solution)/shard_map/all_gather | solution.py:38
  28.3 78.4 %all-gather.10.cloned.1.call-start = ((), (), s32[]{:S(2)}) async-start(), calls=%async_computation.8 | async-start | bytes 1179648 | tf_op jit(solution)/shard_map/all_gather | solution.py:78
  62.2 17.3 %copy-start.22 = (f32[32]{0:T(128)}, f32[32]{0:T(128)S(1)}, u32[]{:S(2)}) copy-start(f32[32]{0:T(128)S(1)} %get-tuple-element.57) | copy-start | bytes 388
  63.9 166.5 %all-gather.12.cloned.1.call-start = ((), (), s32[]{:S(2)}) async-start(), calls=%async_computation.9 | async-start | bytes 15728640 | tf_op jit(solution)/shard_map/all_gather | solution.py:39
  64.5 42.2 %copy-start.19 = (bf16[2048,16]{0,1:T(8,128)(2,1)S(1)}, bf16[2048,16]{0,1:T(8,128)(2,1)}, u32[]{:S(2)}) copy-start(bf16[2048,16]{0,1:T(8,128)(2,1)} %param.15) | copy-start | bytes 196612
  64.5 237.6 %all-gather.14.cloned.1.call-start = ((), (), s32[]{:S(2)}) async-start(), calls=%async_computation.10 | async-start | bytes 7864320 | tf_op jit(solution)/shard_map/all_gather | solution.py:40
  65.1 289.1 %reduce-scatter.8.cloned.1.call-start = ((), (), s32[]{:S(2)}) async-start(), calls=%async_computation.13 | async-start | bytes 1179648 | tf_op jit(solution)/shard_map/reduce_scatter | solution.py:106
  108.3 231.9 %copy-start.20 = (f32[256,16]{0,1:T(8,128)}, f32[256,16]{0,1:T(8,128)S(1)}, u32[]{:S(2)}) copy-start(f32[256,16]{0,1:T(8,128)S(1)} %fusion.107) | copy-start | bytes 49156
  321.4 66.6 %reduce-scatter.6.cloned.1.call-start = ((), (), s32[]{:S(2)}) async-start(), calls=%async_computation.11 | async-start | bytes 1179648 | tf_op jit(solution)/shard_map/reduce_scatter | solution.py:116
  321.5 18.8 %copy-start.4 = (bf16[32,2048]{1,0:T(8,128)(2,1)S(1)}, bf16[32,2048]{1,0:T(8,128)(2,1)}, u32[]{:S(2)}) copy-start(bf16[32,2048]{1,0:T(8,128)(2,1)} %multiply_convert_fusion.6) | copy-start | bytes 393220
  321.5 32.7 %copy-start.3 = (bf16[32,2048]{1,0:T(8,128)(2,1)S(1)}, bf16[32,2048]{1,0:T(8,128)(2,1)}, u32[]{:S(2)}) copy-start(bf16[32,2048]{1,0:T(8,128)(2,1)} %reduce-scatter.4.cloned.1.call-done) | copy-start | bytes 393220
  328.5 120.6 %all-gather.24.cloned.1.call-start = ((), (), s32[]{:S(2)}) async-start(), calls=%async_computation.17 | async-start | bytes 5242880 | tf_op jit(solution)/shard_map/all_gather | solution.py:41
  329.9 10.2 %all-to-all-start = ((f32[2,8,32]{2,0,1:T(2,128)}), f32[2,8,32]{2,0,1:T(2,128)S(1)}, u32[]{:S(2)}, u32[]{:S(2)}) async-start(f32[2,8,32]{2,0,1:T(2,128)} %copy.52), calls=%async_computation.3 | async-start | bytes 16384 | tf_op jit(solution)/shard_map/all_to_all | solution.py:115
  334.5 245.4 %all-reduce.2.cloned.1.call-start = ((), (), s32[]{:S(2)}) async-start(), calls=%async_computation.18 | async-start | bytes 393216 | tf_op jit(solution)/shard_map/psum | solution.py:142
  357.9 247.3 %all-gather.18.cloned.1.call-start = ((), (), s32[]{:S(2)}) async-start(), calls=%async_computation.14 | async-start | bytes 1179648 | tf_op jit(solution)/shard_map/all_gather | solution.py:148
  388.0 6.0 copy-start.32
  388.0 6.0 copy-start.40
  389.9 261.7 %all-gather.20.cloned.1.call-start = ((), (), s32[]{:S(2)}) async-start(), calls=%async_computation.15 | async-start | bytes 1310720 | tf_op jit(solution)/shard_map/all_gather | solution.py:66
  391.5 332.0 %all-gather.22.cloned.1.call-start = ((), (), s32[]{:S(2)}) async-start(), calls=%async_computation.16 | async-start | bytes 7864320 | tf_op jit(solution)/shard_map/all_gather | solution.py:102
  394.0 8.2 %copy-start.26 = (f32[256]{0:T(256)S(1)}, f32[256]{0:T(256)}, u32[]{:S(2)}) copy-start(f32[256]{0:T(256)} %copy-done.25) | copy-start | bytes 3076
  394.0 8.2 %copy-start.34 = (f32[256]{0:T(256)S(1)}, f32[256]{0:T(256)}, u32[]{:S(2)}) copy-start(f32[256]{0:T(256)} %copy-done.33) | copy-start | bytes 3076
  394.0 8.8 %copy-start.28 = (f32[256]{0:T(256)S(1)}, f32[256]{0:T(256)}, u32[]{:S(2)}) copy-start(f32[256]{0:T(256)} %copy-done.27) | copy-start | bytes 3076
  394.0 8.8 %copy-start.36 = (f32[256]{0:T(256)S(1)}, f32[256]{0:T(256)}, u32[]{:S(2)}) copy-start(f32[256]{0:T(256)} %copy-done.35) | copy-start | bytes 3076
  394.0 9.3 %copy-start.30 = (f32[256]{0:T(256)S(1)}, f32[256]{0:T(256)}, u32[]{:S(2)}) copy-start(f32[256]{0:T(256)} %copy-done.29) | copy-start | bytes 3076
  394.0 9.3 %copy-start.38 = (f32[256]{0:T(256)S(1)}, f32[256]{0:T(256)}, u32[]{:S(2)}) copy-start(f32[256]{0:T(256)} %copy-done.37) | copy-start | bytes 3076
  394.0 9.9 %copy-start.1 = (bf16[256,2048]{1,0:T(8,128)(2,1)S(1)}, bf16[256,2048]{1,0:T(8,128)(2,1)}, u32[]{:S(2)}) copy-start(bf16[256,2048]{1,0:T(8,128)(2,1)} %all-gather.10.cloned.1.call-done) | copy-start | bytes 3145732
  397.7 20.7 %all-to-all-start.3 = ((bf16[2,768,256]{2,0,1:T(2,128)(2,1)}), bf16[2,768,256]{2,0,1:T(2,128)(2,1)}, u32[]{:S(2)}, u32[]{:S(2)}) async-start(bf16[2,768,256]{2,0,1:T(2,128)(2,1)} %copy.61), calls=%async_computation.6 | async-start | bytes 1572864 | tf_op jit(solution)/shard_map/all_to_all | solution.py:123
  607.5 6.4 copy-start.13
  607.5 6.4 copy-start.15
  607.5 7.1 copy-start.10
  607.5 21.6 %all-to-all-start.1 = ((bf16[256,4,512]{2,0,1:T(8,128)(2,1)}), bf16[256,4,512]{2,0,1:T(8,128)(2,1)}, u32[]{:S(2)}, u32[]{:S(2)}) async-start(bf16[256,4,512]{2,0,1:T(8,128)(2,1)} %bitcast.83), calls=%async_computation.4 | async-start | bytes 2097152 | tf_op jit(solution)/shard_map/all_to_all | solution.py:149
  614.6 18.7 %copy-start.18 = (bf16[256,512]{0,1:T(8,128)(2,1)S(1)}, bf16[256,512]{0,1:T(8,128)(2,1)}, u32[]{:S(2)}) copy-start(bf16[256,512]{0,1:T(8,128)(2,1)} %copy-done.17) | copy-start | bytes 786436
  616.2 19.6 %copy-start.6 = (f32[256,1024]{0,1:T(8,128)S(1)}, f32[256,1024]{0,1:T(8,128)}, u32[]{:S(2)}) copy-start(f32[256,1024]{0,1:T(8,128)} %copy-done.5) | copy-start | bytes 3145732
  616.2 19.6 %copy-start.41 = (f32[256]{0:T(256)S(1)}, f32[256]{0:T(256)}, u32[]{:S(2)}) copy-start(f32[256]{0:T(256)} %log_add_fusion) | copy-start | bytes 3076
  629.0 25.8 %all-to-all-start.2 = ((bf16[256,4,512]{2,0,1:T(8,128)(2,1)}), bf16[256,4,512]{2,0,1:T(8,128)(2,1)}, u32[]{:S(2)}, u32[]{:S(2)}) async-start(bf16[256,4,512]{2,0,1:T(8,128)(2,1)} %bitcast.82), calls=%async_computation.5 | async-start | bytes 2097152 | tf_op jit(solution)/shard_map/all_to_all | solution.py:79
  (11 other events, 13.7 us)
Sparse Core Ops, SparseCore 0:
  27.6 32.8 reduce-scatter.3
  62.1 20.3 all-gather.15
  84.7 21.9 all-gather.9
  108.3 121.9 all-gather.11
  232.0 70.0 all-gather.13
  321.6 32.5 reduce-scatter.7
  357.0 30.9 reduce-scatter.5
  389.9 59.2 all-gather.23
  455.3 124.6 all-reduce.1
  582.0 23.1 all-gather.17
  607.0 44.5 all-gather.19
  653.9 69.5 all-gather.21
where the time goes:
time: 747 us; the launch traced here: 746 us
  waiting for transfers between devices  573 us (77%)
  matrix products  74 us (10%)
  blocking collectives  25.9 us (3%)
  local copies, waits for them, and re-layouts  21.9 us (3%)
  other arithmetic  18.3 us (2%)
  starting transfers between devices  18.1 us (2%)
  between operations  14.8 us (2%)
    psum x1, waiting for transfers between devices, per_device(): lax.psum(jnp.concatenate([router_term, gain_term], axis=0), ('ctx', 'exp'))  125 us
    all_gather x1, waiting for transfers between devices, per_device(): gate_up_full = lax.all_gather(expert_gate_up, 'ctx', axis=1, tiled=True)  122 us
    all_gather x1, waiting for transfers between devices, per_device(): pair_grad_all = lax.all_gather(pair_grad, 'ctx', axis=1, tiled=True)  68.7 us
    all_gather x1, waiting for transfers between devices, per_device(): down_full = lax.all_gather(expert_down, 'ctx', axis=1, tiled=True)  61.8 us
    reduce_scatter x1, waiting for transfers between devices, per_device(): lax.psum_scatter(jnp.dot(attention_flat, out_weight, preferred_element_ty...  32.2 us
    reduce_scatter x1, waiting for transfers between devices, per_device(): lax.psum_scatter(jnp.sum(probs_cols * expert_out, axis=0).astype(jnp.bflo...  30.1 us
    all_gather x1, waiting for transfers between devices, per_device(): upstream_all = lax.all_gather(upstream_block, 'ctx', axis=0, tiled=True)  29.4 us
    all_gather x1, waiting for transfers between devices, per_device(): arriving = lax.all_gather(input_grad, 'exp', axis=0, tiled=True)  22.2 us
  transfers between devices with their start and end apart: 16, of which 15 were waited for; matrix products, arithmetic and copies ran while one was open for 9% of the time, Pallas kernels for 0%

commit v1 on v0

--- a/solution.py
+++ b/solution.py
@@ -139,7 +139,9 @@
         "te,de->td", logit_grad, router_weight.astype(jnp.float32), precision=lax.Precision.HIGHEST
     )
     gain_term = jnp.sum(normed_grad * residual * inv_rms, axis=0, keepdims=True)
-    summed = lax.psum(jnp.concatenate([router_term, gain_term], axis=0), ("ctx", "exp"))
+    summed = jnp.sum(
+        lax.all_gather(jnp.concatenate([router_term, gain_term], axis=0), ("ctx", "exp")), axis=0
+    )
     router_grad, gain_grad = (summed[:EXPERTS].T, summed[EXPERTS])
     inner_mean = jnp.mean(residual * norm_gain * normed_grad, axis=1, keepdims=True)
     input_grad = (

time: 747 us -> 673 us (0.901)
  waiting for transfers between devices: 573 us -> 499 us
    psum x1 -> x0, waiting for transfers between devices: 125 us -> none  [per_device(): lax.psum(jnp.concatenate([router_term, gain_term], axis=0), ('ctx', 'exp'))]
    all_gather x0 -> x1, waiting for transfers between devices: none -> 56.5 us  [per_device(): lax.all_gather(jnp.concatenate([router_term, gain_term], axis=0), ('ctx',...]
  transfers between devices with their start and end apart: 16 -> 16, of which waited for: 15 -> 15; matrix products, arithmetic and copies ran while one was open for 9% -> 12% of each run, Pallas kernels for 0% -> 0%
where the time goes in v1:
time: 673 us; the launch traced here: 672 us
  waiting for transfers between devices  499 us (74%)
  matrix products  74.1 us (11%)
  blocking collectives  25.8 us (4%)
  local copies, waits for them, and re-layouts  20.3 us (3%)
  other arithmetic  19.5 us (3%)
  starting transfers between devices  18.1 us (3%)
  between operations  14.8 us (2%)
    all_gather x1, waiting for transfers between devices, per_device(): gate_up_full = lax.all_gather(expert_gate_up, 'ctx', axis=1, tiled=True)  122 us
    all_gather x1, waiting for transfers between devices, per_device(): pair_grad_all = lax.all_gather(pair_grad, 'ctx', axis=1, tiled=True)  69.9 us
    all_gather x1, waiting for transfers between devices, per_device(): down_full = lax.all_gather(expert_down, 'ctx', axis=1, tiled=True)  61.8 us
    all_gather x1, waiting for transfers between devices, per_device(): lax.all_gather(jnp.concatenate([router_term, gain_term], axis=0), ('ctx',...  56.5 us
    reduce_scatter x1, waiting for transfers between devices, per_device(): lax.psum_scatter(jnp.sum(probs_cols * expert_out, axis=0).astype(jnp.bflo...  32.4 us
    reduce_scatter x1, waiting for transfers between devices, per_device(): lax.psum_scatter(jnp.dot(attention_flat, out_weight, preferred_element_ty...  32.2 us
    all_gather x1, waiting for transfers between devices, per_device(): upstream_all = lax.all_gather(upstream_block, 'ctx', axis=0, tiled=True)  29.4 us
    all_gather x1, waiting for transfers between devices, per_device(): normed_block = lax.all_gather(normed, 'exp', axis=0, tiled=True)  21.3 us
  transfers between devices with their start and end apart: 16, of which 15 were waited for; matrix products, arithmetic and copies ran while one was open for 12% of the time, Pallas kernels for 0%

profile of v1, /device:TPU:0, one launch (start us, length us, event | category | flops | bytes accessed | tf_op | source)
XLA Modules:
  0.0 671.7 jit_solution(9229757774867903891)
XLA Ops:
  8.3 11.5 %all_gather.36 = bf16[1024,256]{1,0:T(8,128)(2,1)S(1)} all-gather(bf16[256,256]{1,0:T(8,128)(2,1)S(1)} %constant_dynamic-slice_fusion), channel_id=1, replica_groups=mesh['ctx'=4,'exp'=8] {'ctx'}, dimensions={0}, use_global_device_ids=true | all-gather | bytes 655360 | tf_op jit(solution)/shard_map/all_gather | solution.py:36
  19.9 1.3 fusion.115
  21.1 1.3 fusion.114
  25.6 1.7 convolution_convert_fusion.1
  28.1 32.2 %reduce-scatter.4.cloned.1.call-done = bf16[32,2048]{1,0:T(8,128)(2,1)} async-done(((bf16[256,2048]{1,0:T(8,128)(2,1)}), bf16[32,2048]{1,0:T(8,128)(2,1)}) %reduce-scatter.4.cloned.1.call-update) | async-done | bytes 131088 | tf_op jit(solution)/shard_map/reduce_scatter | solution.py:67
  61.4 1.7 multiply_convert_fusion.6
  64.4 14.3 %all-gather.1 = s32[8,32,8]{1,2,0:T(8,128)S(1)} all-gather(s32[1,32,8]{1,2,0:T(8,128)S(1)} %bitcast.95), channel_id=1, replica_groups=mesh['ctx'=4,'exp'=8] {'exp'}, dimensions={0}, use_global_device_ids=true | all-gather | bytes 9216 | tf_op jit(solution)/shard_map/all_gather | solution.py:37
  78.7 3.8 all-gather.19.cloned.1.call-done
  82.5 2.8 convert_element_type.151
  85.3 21.3 %all-gather.13.cloned.1.call-done = bf16[256,2048]{1,0:T(8,128)(2,1)} async-done(((bf16[32,2048]{1,0:T(8,128)(2,1)}), bf16[256,2048]{1,0:T(8,128)(2,1)}) %all-gather.13.cloned.1.call-update) | async-done | bytes 1048592 | tf_op jit(solution)/shard_map/all_gather | solution.py:78
  106.6 1.6 fusion.116
  108.3 122.0 %all-gather.15.cloned.1.call-done = bf16[2,2048,1536]{2,1,0:T(8,128)(2,1)} async-done(((bf16[2,512,1536]{2,1,0:T(8,128)(2,1)}), bf16[2,2048,1536]{2,1,0:T(8,128)(2,1)}) %all-gather.15.cloned.1.call-update) | async-done | bytes 12582928 | tf_op jit(solution)/shard_map/all_gather | solution.py:39
  230.4 10.0 %convolution_bitcast_fusion.1 = f32[2,256,1536]{2,1,0:T(8,128)} fusion(bf16[2,2048,1536]{2,1,0:T(8,128)(2,1)} %all-gather.15.cloned.1.call-done, bf16[256,2048]{1,0:T(8,128)(2,1)} %all-gather.13.cloned.1.call-done), kind=kOutput, calls=%fused_computation.8 | convolution fusion | flops 3221225472 | bytes 16777216 | tf_op jit(solution)/shard_map/td,edf->etf/dot_general | solution.py:90
  240.3 61.8 %all-gather.17.cloned.1.call-done = bf16[2,768,2048]{2,1,0:T(8,128)(2,1)} async-done(((bf16[2,192,2048]{2,1,0:T(8,128)(2,1)}), bf16[2,768,2048]{2,1,0:T(8,128)(2,1)}) %all-gather.17.cloned.1.call-update) | async-done | bytes 6291472 | tf_op jit(solution)/shard_map/all_gather | solution.py:40
  302.1 9.4 %multiply_convert_fusion.4 = (bf16[2,256,768]{2,1,0:T(8,128)(2,1)S(1)}, bf16[2,256,768]{2,1,0:T(8,128)(2,1)S(1)}, bf16[2,768,256]{1,2,0:T(8,128)(2,1)}, bf16[2,256,768]{2,1,0:T(8,128)(2,1)}) fusion(f32[2,256,1536]{2,1,0:T(8,128)} %convolution_bitcast_fusion.1, f32[2,256]{1,0:T(2,128)S(1)} %dynamic-slice_bitcast_fusion, ...), kind=kOutput, calls=%fused_computation.20 | convolution fusion | flops 1620180992 | bytes 14684160 | tf_op jit(solution)/shard_map/etd,efd->etf/dot_general | solution.py:98
  312.7 9.0 %fusion.4 = bf16[256,2048]{1,0:T(8,128)(2,1)} fusion(bf16[2,2048,1536]{2,1,0:T(8,128)(2,1)} %all-gather.15.cloned.1.call-done, bf16[2,256,768]{2,1,0:T(8,128)(2,1)S(1)} %get-tuple-element.51, bf16[2,256,768]{2,1,0:T(8,128)(2,1)S(1)} %get-tuple-element.50), kind=kOutput, calls=%fused_computation.12 | convolution fusion | flops 3224895488 | bytes 15204352 | tf_op jit(solution)/shard_map/etf,edf->td/dot_general | solution.py:103
  321.8 7.0 %fusion.1 = (f32[2,256]{1,0:T(2,128)S(1)}, bf16[256,2048]{1,0:T(8,128)(2,1)}) fusion(f32[256,2048]{1,0:T(8,128)} %convert_element_type.151, f32[2,256]{1,0:T(2,128)S(1)} %dynamic-slice_bitcast_fusion, bf16[2,256,768]{2,1,0:T(8,128)(2,1)} %get-tuple-element.53, bf16[2,768,2048]{2,1,0:T(8,128)(2,1)} %all-gather.17.cloned.1.call-done), kind=kOutput, calls=%fused_computation.4 | convolution fusion | flops 1616379392 | bytes 10227712 | tf_op jit(solution)/shard_map/etf,efd->etd/dot_general | solution.py:110
  330.2 4.6 all-to-all-start
  334.9 5.6 all-to-all-done
  340.5 13.9 %reduce-scatter.8.cloned.1.call-done = bf16[32,2048]{1,0:T(8,128)(2,1)} async-done(((bf16[256,2048]{1,0:T(8,128)(2,1)}), bf16[32,2048]{1,0:T(8,128)(2,1)}) %reduce-scatter.8.cloned.1.call-update) | async-done | bytes 131088 | tf_op jit(solution)/shard_map/reduce_scatter | solution.py:106
  354.5 1.5 multiply_reduce_fusion
  356.0 32.4 %reduce-scatter.6.cloned.1.call-done = bf16[32,2048]{1,0:T(8,128)(2,1)} async-done(((bf16[256,2048]{1,0:T(8,128)(2,1)}), bf16[32,2048]{1,0:T(8,128)(2,1)}) %reduce-scatter.6.cloned.1.call-update) | async-done | bytes 131088 | tf_op jit(solution)/shard_map/reduce_scatter | solution.py:116
  388.4 1.8 subtract_convert_fusion
  391.0 2.6 pad_maximum_fusion
  395.6 1.2 log_add_fusion.3
  396.8 3.0 copy.61
  399.8 4.4 all-to-all-start.3
  407.1 11.6 %all-to-all-done.3 = bf16[2,768,256]{2,0,1:T(2,128)(2,1)} async-done(((bf16[2,768,256]{2,0,1:T(2,128)(2,1)}), bf16[2,768,256]{2,0,1:T(2,128)(2,1)}, u32[]{:S(2)}, u32[]{:S(2)}) %all-to-all-start.3) | async-done | bytes 786464 | tf_op jit(solution)/shard_map/all_to_all | solution.py:123
  418.7 1.2 copy.62
  420.0 29.4 %all-gather.27.cloned.1.call-done = bf16[1024,2048]{1,0:T(8,128)(2,1)} async-done(((bf16[256,2048]{1,0:T(8,128)(2,1)}), bf16[1024,2048]{1,0:T(8,128)(2,1)}) %all-gather.27.cloned.1.call-update) | async-done | bytes 4194320 | tf_op jit(solution)/shard_map/all_gather | solution.py:41
  449.5 5.6 fusion.2
  455.1 18.8 %all-gather.21.cloned.1.call-done = bf16[256,2048]{1,0:T(8,128)(2,1)} async-done(((bf16[32,2048]{1,0:T(8,128)(2,1)}), bf16[256,2048]{1,0:T(8,128)(2,1)}) %all-gather.21.cloned.1.call-update) | async-done | bytes 1048592 | tf_op jit(solution)/shard_map/all_gather | solution.py:150
  473.9 2.3 copy.78
  476.2 4.4 all-to-all-start.1
  480.6 2.0 convolution_convert_fusion.2
  483.3 1.6 fusion.39
  485.0 2.0 fusion.38
  487.0 10.8 %all-to-all-done.1 = bf16[256,4,512]{2,0,1:T(8,128)(2,1)} async-done(((bf16[256,4,512]{2,0,1:T(8,128)(2,1)}), bf16[256,4,512]{2,0,1:T(8,128)(2,1)}, u32[]{:S(2)}, u32[]{:S(2)}) %all-to-all-start.1) | async-done | bytes 1048608 | tf_op jit(solution)/shard_map/all_to_all | solution.py:151
  497.8 4.3 all-to-all-start.2
  502.0 2.5 fusion.37
  504.6 2.2 fusion.36
  508.5 6.5 all-gather.23.cloned.1.call-done
  515.1 3.2 fusion.117
  518.3 69.9 %all-gather.25.cloned.1.call-done = bf16[2,1024,1536]{2,1,0:T(8,128)(2,1)} async-done(((bf16[2,256,1536]{2,1,0:T(8,128)(2,1)}), bf16[2,1024,1536]{2,1,0:T(8,128)(2,1)}) %all-gather.25.cloned.1.call-update) | async-done | bytes 6291472 | tf_op jit(solution)/shard_map/all_gather | solution.py:102
  588.2 9.1 %convolution_bitcast_fusion = f32[2,512,1536]{1,2,0:T(8,128)} fusion(bf16[2,1024,1536]{2,1,0:T(8,128)(2,1)} %all-gather.25.cloned.1.call-done, bf16[1024,512,1]{1,0,2:T(8,128)(2,1)} %bitcast.18), kind=kOutput, calls=%fused_computation.2 | convolution fusion | flops 3221225472 | bytes 13631488 | tf_op jit(solution)/shard_map/td,etf->edf/dot_general | solution.py:129
  597.3 6.6 copy.65
  603.9 56.5 %all-gather.29.cloned.1.call-done = f32[32,17,2048]{2,1,0:T(8,128)} async-done(((f32[1,17,2048]{2,1,0:T(8,128)}), f32[32,17,2048]{2,1,0:T(8,128)}) %all-gather.29.cloned.1.call-update) | async-done | bytes 4456464 | tf_op jit(solution)/shard_map/all_gather | solution.py:143
  660.4 3.2 reduce_sum.159
  (138 shorter events, 19.4 us)
Async XLA Ops:
  7.2 18.4 %copy-start = (bf16[512,2048]{1,0:T(8,128)(2,1)S(1)}, bf16[512,2048]{1,0:T(8,128)(2,1)}, u32[]{:S(2)}) copy-start(bf16[512,2048]{1,0:T(8,128)(2,1)} %param.13) | copy-start | bytes 6291460
  7.2 15.2 %copy-start.37 = (bf16[256,512]{1,0:T(8,128)(2,1)S(1)}, bf16[256,512]{1,0:T(8,128)(2,1)}, u32[]{:S(2)}) copy-start(bf16[256,512]{1,0:T(8,128)(2,1)} %param.11) | copy-start | bytes 786436
  7.2 53.2 %reduce-scatter.4.cloned.1.call-start = ((), (), s32[]{:S(2)}) async-start(), calls=%async_computation.7 | async-start | bytes 1179648 | tf_op jit(solution)/shard_map/reduce_scatter | solution.py:67
  19.9 5.3 copy-start.13
  21.1 2.6 copy-start.9
  21.1 2.6 copy-start.28
  22.4 1.6 copy-start.8
  22.8 1.8 copy-start.7
  22.8 1.8 copy-start.24
  23.2 2.0 copy-start.5
  23.2 2.0 copy-start.26
  24.6 2.7 copy-start.31
  25.2 36.2 %copy-start.33 = (f32[256]{0:T(256)}, f32[256]{0:T(256)S(1)}, u32[]{:S(2)}) copy-start(f32[256]{0:T(256)S(1)} %fusion.55) | copy-start | bytes 3076
  25.2 35.1 %copy-start.2 = (bf16[32,2048]{1,0:T(8,128)(2,1)S(1)}, bf16[32,2048]{1,0:T(8,128)(2,1)}, u32[]{:S(2)}) copy-start(bf16[32,2048]{1,0:T(8,128)(2,1)} %param.10) | copy-start | bytes 393220
  25.2 36.2 %copy-start.19 = (f32[2048]{0:T(1024)S(1)}, f32[2048]{0:T(1024)}, u32[]{:S(2)}) copy-start(f32[2048]{0:T(1024)} %param.14) | copy-start | bytes 24580
  27.3 37.1 %copy-start.21 = (s32[32,8]{0,1:T(8,128)S(1)}, s32[32,8]{0,1:T(8,128)}, u32[]{:S(2)}) copy-start(s32[32,8]{0,1:T(8,128)} %param.18) | copy-start | bytes 3076
  27.3 55.2 %all-gather.19.cloned.1.call-start = ((), (), s32[]{:S(2)}) async-start(), calls=%async_computation.12 | async-start | bytes 1179648 | tf_op jit(solution)/shard_map/all_gather | solution.py:38
  28.1 78.6 %all-gather.13.cloned.1.call-start = ((), (), s32[]{:S(2)}) async-start(), calls=%async_computation.8 | async-start | bytes 1179648 | tf_op jit(solution)/shard_map/all_gather | solution.py:78
  63.1 167.2 %all-gather.15.cloned.1.call-start = ((), (), s32[]{:S(2)}) async-start(), calls=%async_computation.9 | async-start | bytes 15728640 | tf_op jit(solution)/shard_map/all_gather | solution.py:39
  63.7 42.9 %copy-start.17 = (bf16[2048,16]{0,1:T(8,128)(2,1)S(1)}, bf16[2048,16]{0,1:T(8,128)(2,1)}, u32[]{:S(2)}) copy-start(bf16[2048,16]{0,1:T(8,128)(2,1)} %param.15) | copy-start | bytes 196612
  63.7 238.4 %all-gather.17.cloned.1.call-start = ((), (), s32[]{:S(2)}) async-start(), calls=%async_computation.10 | async-start | bytes 7864320 | tf_op jit(solution)/shard_map/all_gather | solution.py:40
  64.3 290.2 %reduce-scatter.8.cloned.1.call-start = ((), (), s32[]{:S(2)}) async-start(), calls=%async_computation.13 | async-start | bytes 1179648 | tf_op jit(solution)/shard_map/reduce_scatter | solution.py:106
  108.3 246.2 %copy-start.18 = (f32[256,16]{0,1:T(8,128)}, f32[256,16]{0,1:T(8,128)S(1)}, u32[]{:S(2)}) copy-start(f32[256,16]{0,1:T(8,128)S(1)} %fusion.107) | copy-start | bytes 49156
  321.7 66.6 %reduce-scatter.6.cloned.1.call-start = ((), (), s32[]{:S(2)}) async-start(), calls=%async_computation.11 | async-start | bytes 1179648 | tf_op jit(solution)/shard_map/reduce_scatter | solution.py:116
  321.8 32.7 %copy-start.3 = (bf16[32,2048]{1,0:T(8,128)(2,1)S(1)}, bf16[32,2048]{1,0:T(8,128)(2,1)}, u32[]{:S(2)}) copy-start(bf16[32,2048]{1,0:T(8,128)(2,1)} %reduce-scatter.4.cloned.1.call-done) | copy-start | bytes 393220
  321.8 66.6 %copy-start.14 = (bf16[32,2048]{1,0:T(8,128)(2,1)S(1)}, bf16[32,2048]{1,0:T(8,128)(2,1)}, u32[]{:S(2)}) copy-start(bf16[32,2048]{1,0:T(8,128)(2,1)} %param.19) | copy-start | bytes 393220
  328.8 120.7 %all-gather.27.cloned.1.call-start = ((), (), s32[]{:S(2)}) async-start(), calls=%async_computation.17 | async-start | bytes 5242880 | tf_op jit(solution)/shard_map/all_gather | solution.py:41
  330.2 10.2 %all-to-all-start = ((f32[2,8,32]{2,0,1:T(2,128)}), f32[2,8,32]{2,0,1:T(2,128)S(1)}, u32[]{:S(2)}, u32[]{:S(2)}) async-start(f32[2,8,32]{2,0,1:T(2,128)} %copy.52), calls=%async_computation.3 | async-start | bytes 16384 | tf_op jit(solution)/shard_map/all_to_all | solution.py:115
  334.8 139.1 %all-gather.21.cloned.1.call-start = ((), (), s32[]{:S(2)}) async-start(), calls=%async_computation.14 | async-start | bytes 1179648 | tf_op jit(solution)/shard_map/all_gather | solution.py:150
  340.5 50.5 %copy-start.20 = (f32[32]{0:T(128)}, f32[32]{0:T(128)S(1)}, u32[]{:S(2)}) copy-start(f32[32]{0:T(128)S(1)} %multiply_reduce_fusion.7) | copy-start | bytes 388
  388.4 5.4 copy-start.4
  390.1 124.9 %all-gather.23.cloned.1.call-start = ((), (), s32[]{:S(2)}) async-start(), calls=%async_computation.15 | async-start | bytes 1310720 | tf_op jit(solution)/shard_map/all_gather | solution.py:66
  391.0 197.2 %all-gather.25.cloned.1.call-start = ((), (), s32[]{:S(2)}) async-start(), calls=%async_computation.16 | async-start | bytes 7864320 | tf_op jit(solution)/shard_map/all_gather | solution.py:102
  393.6 12.3 %copy-start.1 = (bf16[256,2048]{1,0:T(8,128)(2,1)S(1)}, bf16[256,2048]{1,0:T(8,128)(2,1)}, u32[]{:S(2)}) copy-start(bf16[256,2048]{1,0:T(8,128)(2,1)} %all-gather.13.cloned.1.call-done) | copy-start | bytes 3145732
  393.7 266.7 %all-gather.29.cloned.1.call-start = ((), (), s32[]{:S(2)}) async-start(), calls=%async_computation.18 | async-start | bytes 6488064 | tf_op jit(solution)/shard_map/all_gather | solution.py:143
  394.8 9.5 %copy-start.23 = (f32[256]{0:T(256)S(1)}, f32[256]{0:T(256)}, u32[]{:S(2)}) copy-start(f32[256]{0:T(256)} %copy-done.22) | copy-start | bytes 3076
  394.8 9.5 %copy-start.30 = (f32[256]{0:T(256)S(1)}, f32[256]{0:T(256)}, u32[]{:S(2)}) copy-start(f32[256]{0:T(256)} %copy-done.29) | copy-start | bytes 3076
  394.8 10.0 %copy-start.25 = (f32[256]{0:T(256)S(1)}, f32[256]{0:T(256)}, u32[]{:S(2)}) copy-start(f32[256]{0:T(256)} %copy-done.24) | copy-start | bytes 3076
  394.8 10.0 %copy-start.32 = (f32[256]{0:T(256)S(1)}, f32[256]{0:T(256)}, u32[]{:S(2)}) copy-start(f32[256]{0:T(256)} %copy-done.31) | copy-start | bytes 3076
  394.8 10.6 %copy-start.27 = (f32[256]{0:T(256)S(1)}, f32[256]{0:T(256)}, u32[]{:S(2)}) copy-start(f32[256]{0:T(256)} %copy-done.26) | copy-start | bytes 3076
  394.8 10.6 %copy-start.34 = (f32[256]{0:T(256)S(1)}, f32[256]{0:T(256)}, u32[]{:S(2)}) copy-start(f32[256]{0:T(256)} %copy-done.33) | copy-start | bytes 3076
  399.8 18.9 %all-to-all-start.3 = ((bf16[2,768,256]{2,0,1:T(2,128)(2,1)}), bf16[2,768,256]{2,0,1:T(2,128)(2,1)}, u32[]{:S(2)}, u32[]{:S(2)}) async-start(bf16[2,768,256]{2,0,1:T(2,128)(2,1)} %copy.61), calls=%async_computation.6 | async-start | bytes 1572864 | tf_op jit(solution)/shard_map/all_to_all | solution.py:123
  476.2 7.1 %copy-start.10 = (f32[256,1024]{0,1:T(8,128)S(1)}, f32[256,1024]{0,1:T(8,128)}, u32[]{:S(2)}) copy-start(f32[256,1024]{0,1:T(8,128)} %copy-done.9) | copy-start | bytes 3145732
  476.2 21.6 %all-to-all-start.1 = ((bf16[256,4,512]{2,0,1:T(8,128)(2,1)}), bf16[256,4,512]{2,0,1:T(8,128)(2,1)}, u32[]{:S(2)}, u32[]{:S(2)}) async-start(bf16[256,4,512]{2,0,1:T(8,128)(2,1)} %bitcast.85), calls=%async_computation.4 | async-start | bytes 2097152 | tf_op jit(solution)/shard_map/all_to_all | solution.py:151
  483.3 18.7 %copy-start.16 = (bf16[256,512]{0,1:T(8,128)(2,1)S(1)}, bf16[256,512]{0,1:T(8,128)(2,1)}, u32[]{:S(2)}) copy-start(bf16[256,512]{0,1:T(8,128)(2,1)} %copy-done.15) | copy-start | bytes 786436
  485.0 19.6 %copy-start.6 = (f32[256,1024]{0,1:T(8,128)S(1)}, f32[256,1024]{0,1:T(8,128)}, u32[]{:S(2)}) copy-start(f32[256,1024]{0,1:T(8,128)} %copy-done.5) | copy-start | bytes 3145732
  485.0 19.6 %copy-start.36 = (f32[256]{0:T(256)S(1)}, f32[256]{0:T(256)}, u32[]{:S(2)}) copy-start(f32[256]{0:T(256)} %log_add_fusion) | copy-start | bytes 3076
  497.8 20.5 %all-to-all-start.2 = ((bf16[256,4,512]{2,0,1:T(8,128)(2,1)}), bf16[256,4,512]{2,0,1:T(8,128)(2,1)}, u32[]{:S(2)}, u32[]{:S(2)}) async-start(bf16[256,4,512]{2,0,1:T(8,128)(2,1)} %bitcast.84), calls=%async_computation.5 | async-start | bytes 2097152 | tf_op jit(solution)/shard_map/all_to_all | solution.py:79
  (6 other events, 7.4 us)
Sparse Core Ops, SparseCore 0:
  27.4 32.8 reduce-scatter.3
  62.0 20.5 all-gather.18
  84.7 21.8 all-gather.12
  108.3 121.9 all-gather.14
  232.0 70.0 all-gather.16
  321.8 32.5 reduce-scatter.7
  357.3 30.9 reduce-scatter.5
  390.2 59.2 all-gather.26
  451.6 22.2 all-gather.20
  475.6 39.4 all-gather.22
  517.5 70.6 all-gather.24
  591.1 69.2 all-gather.28
